TPU v7x, 256 devices: a whole 4x4x8 slice. The times are simulated.
256 devices in a mesh: cp: 32 (over z_lo, y, core), tp: 8 (over z_hi, x).
Axes of the slice: x: 4, y: 4, z: 8 (z_hi: 2, z_lo: 4; z = z_hi * 4 + z_lo), core: 2. Of those that a mesh axis runs over, the one named last changes fastest.
Arguments:
- tokens: bfloat16 [16384, 4096], P('cp', 'tp'), may hold values from -40 to 40
- span_ids: int32 [32, 2], P('cp'), may hold values from 0 to 63, as said below
- positions: int32 [16384], P('cp'), may hold values from 0 to 8191, as said below
- q_weight: bfloat16 [4096, 4096], P(None, 'tp'), may hold values from -0.09375 to 0.09375
- k_weight: bfloat16 [4096, 1024], P(None, 'tp'), may hold values from -0.09375 to 0.09375
- v_weight: bfloat16 [4096, 1024], P(None, 'tp'), may hold values from -0.09375 to 0.09375
- o_weight: bfloat16 [4096, 4096], P('tp'), may hold values from -0.09375 to 0.09375
Outputs:
- attended: bfloat16 [16384, 4096], P('cp', 'tp')
Inputs may be any that keep to these rules, and one draw needn't show every extreme that they name: `span_ids`: row r names the two spans held by index r of cp: a span c and the span 64 - 1 - c, in either order; every span is named once. Span c covers the places c * (256) to (c + 1) * 256 - 1 of the sequence. `positions`: along the sequence (in the order of places given by span_ids) documents are runs of consecutive tokens; a position is 0 at a document's first token and rises by one up to its last, and the first place of the sequence has position 0.
All inputs are finite; a program needn't handle non-finite values.
Results may differ from a plain program's by a relative error of at most 0.014.
The roundings to bfloat16 on the way count: a program that leaves them out, or rounds other values in their place, can miss the bound.
Values may be sent and summed in bfloat16 or wider, within the bound.
A program may use at most 64 MiB of HBM per device.

v0:
```python
from functools import partial
import jax
import jax.numpy as jnp
from jax import lax
from jax.sharding import Mesh
from jax.sharding import PartitionSpec as P

HD = 128
TP = ("tp_0", "tp_1")
CP = ("cp_0", "cp_1", "cp_2")
theta_base = 500000.0
floor_score = -1e30


def in_order(pieces, dim):
    shape = list(pieces.shape[1:])
    shape[dim] *= pieces.shape[0]
    return jnp.moveaxis(pieces, 0, dim).reshape(shape)


def all_blocks(value, axes, order):
    pieces = value[None]
    for k in order:
        pieces = lax.all_gather(pieces, axes[k], axis=0, tiled=True)
    current = [lax.axis_size(axes[k]) for k in reversed(order)]
    pieces = pieces.reshape(*current, *value.shape)
    turned = sorted(range(len(order)), key=lambda place: order[len(order) - 1 - place])
    return pieces.transpose(*turned, *range(len(order), pieces.ndim)).reshape(-1, *value.shape)


def gather_axes(value, axes, order, dim):
    return in_order(all_blocks(value, axes, order), dim)


def from_behind(block, axis, distance):
    devices = range(lax.axis_size(axis))
    route = [((i - distance) % len(devices), i) for i in devices]
    return lax.ppermute(block, axis, route)


def sum_in_order(pieces, axes, order):
    inside = pieces.shape[1:]
    pieces = pieces.reshape(*(lax.axis_size(a) for a in axes), *inside)
    pieces = jnp.moveaxis(pieces, order, range(len(axes))).reshape(-1, *inside)
    for k in order:
        pieces = lax.psum_scatter(pieces, axes[k], scatter_dimension=0, tiled=True)
    return pieces[0]


def in_blocks(value, dim, length):
    shape = value.shape
    pieces = value.reshape(*shape[:dim], length, shape[dim] // length, *shape[dim + 1 :])
    return jnp.moveaxis(pieces, dim, 0)


def sum_by_axis(value, axes, order, dim):
    length = lax.axis_size(axes)
    return sum_in_order(in_blocks(value, dim, length), axes, order)


def rotate(vectors, positions):
    half_size = vectors.shape[-1] // 2
    exponent = jnp.arange(half_size, dtype=jnp.float32) * (2.0 / vectors.shape[-1])
    inverse_freq = theta_base ** (-exponent)
    angles = positions.astype(jnp.float32)[:, None] * inverse_freq[None, :]
    cosine = jnp.cos(angles)[:, None, :]
    sine_part = jnp.sin(angles)[:, None, :]
    lower_half = vectors[..., :half_size]
    upper_half = vectors[..., half_size:]
    return jnp.concatenate(
        [
            lower_half * cosine - upper_half * sine_part,
            upper_half * cosine + lower_half * sine_part,
        ],
        axis=-1,
    )


def block_update(
    carried, block_queries, query_index, query_start, block_keys, block_values, key_index
):
    row_max, weight_sum, weighted = carried
    scale_factor = block_queries.shape[-1] ** (-0.5)
    scores = (
        jnp.einsum("hrd,kd->hrk", block_queries, block_keys, preferred_element_type=jnp.float32)
        * scale_factor
    )
    visible = (
        (key_index[None, :] <= query_index[:, None]) & (key_index[None, :] >= query_start[:, None])
    )[None]
    scores = jnp.where(visible, scores, floor_score)
    new_max = jnp.maximum(row_max, jnp.max(scores, axis=-1))
    weights = jnp.where(visible, jnp.exp(scores - new_max[..., None]), 0.0)
    rescale = jnp.exp(row_max - new_max)
    weight_sum = weight_sum * rescale + jnp.sum(weights, axis=-1)
    weighted = weighted * rescale[..., None] + jnp.einsum(
        "hrk,kd->hrd",
        weights.astype(jnp.bfloat16),
        block_values,
        preferred_element_type=jnp.float32,
    )
    return (new_max, weight_sum, weighted)


def keep_state(carried):
    return carried


def attend(halves, query_parts, key_block, value_block, key_index):
    half_rows = key_block.shape[0] // 2
    updated = []
    for query_half in range(2):
        carried = halves[query_half]
        block_queries, query_index, query_start = query_parts[query_half]
        lowest_start = jnp.min(query_start)
        for key_half in range(2):
            key_rows = lax.slice_in_dim(
                key_block, key_half * half_rows, (key_half + 1) * half_rows, axis=0
            )
            value_rows = lax.slice_in_dim(
                value_block, key_half * half_rows, (key_half + 1) * half_rows, axis=0
            )
            index_rows = lax.slice_in_dim(
                key_index, key_half * half_rows, (key_half + 1) * half_rows, axis=0
            )
            needed = (index_rows[0] <= query_index[-1]) & (index_rows[-1] >= lowest_start)
            update_fn = partial(
                block_update,
                block_queries=block_queries,
                query_index=query_index,
                query_start=query_start,
                block_keys=key_rows,
                block_values=value_rows,
                key_index=index_rows,
            )
            carried = lax.cond(needed, update_fn, keep_state, carried)
        updated.append(carried)
    return tuple(updated)


def per_device(tokens, span_ids, positions, q_weight, k_weight, v_weight, o_weight):
    row_count = tokens.shape[0]
    half_rows = row_count // 2
    head_count = q_weight.shape[1] // HD
    weights_in = (q_weight, k_weight, v_weight)
    pieces = lax.all_gather(tokens, TP, axis=1, tiled=True)
    queries, keys_here, values_here = tuple(
        (jnp.dot(pieces, matrix, preferred_element_type=jnp.float32) for matrix in weights_in)
    )
    queries = rotate(queries.reshape(row_count, head_count, HD), positions).astype(jnp.bfloat16)
    queries = jnp.transpose(queries, (1, 0, 2))
    keys_here = (
        rotate(keys_here.reshape(row_count, 1, HD), positions)
        .reshape(row_count, HD)
        .astype(jnp.bfloat16)
    )
    values_here = values_here.astype(jnp.bfloat16)
    span_table = gather_axes(span_ids, (("cp_0", "cp_1"), "cp_2"), (0, 1), 0)
    rank_count = span_table.shape[0]
    offsets = jnp.arange(half_rows, dtype=jnp.int32)
    global_index = (span_table[:, :, None] * half_rows + offsets[None, None, :]).reshape(
        rank_count * row_count
    )
    my_rank = lax.axis_index(CP)
    own_index = lax.dynamic_slice_in_dim(global_index, my_rank * row_count, row_count)
    doc_start = own_index - positions
    query_parts = tuple(
        (
            (
                queries[:, part_index * half_rows : (part_index + 1) * half_rows],
                own_index[part_index * half_rows : (part_index + 1) * half_rows],
                doc_start[part_index * half_rows : (part_index + 1) * half_rows],
            )
            for part_index in range(2)
        )
    )
    empty_state = (
        jnp.full((head_count, half_rows), floor_score, jnp.float32),
        jnp.zeros((head_count, half_rows), jnp.float32),
        jnp.zeros((head_count, half_rows, HD), jnp.float32),
    )
    halves = (empty_state, empty_state)
    halves = attend(halves, query_parts, keys_here, values_here, own_index)

    def turn(turn_index, loop_state):
        carried, moving = loop_state
        moving = from_behind(moving, CP, 1)
        source = (my_rank - turn_index - 1) % rank_count
        key_index = lax.dynamic_slice_in_dim(global_index, source * row_count, row_count)
        return (attend(carried, query_parts, moving[0], moving[1], key_index), moving)

    halves, moved_last = lax.fori_loop(
        0, rank_count - 1, turn, (halves, jnp.stack((keys_here, values_here)))
    )
    outputs = []
    for carried in halves:
        outputs.append(carried[2] / carried[1][..., None])
    attention = jnp.concatenate(outputs, axis=1).astype(jnp.bfloat16)
    out_weight = o_weight.reshape(head_count, HD, o_weight.shape[1])
    partial_sum = jnp.einsum(
        "hrd,hdn->rn", attention, out_weight, preferred_element_type=jnp.float32
    )
    return (
        sum_by_axis(partial_sum.astype(jnp.bfloat16), TP, (1, 0), 1)
        .astype(jnp.float32)
        .astype(jnp.bfloat16)
    )


def solution(mesh):
    split = Mesh(mesh.devices.reshape(4, 4, 2, 2, 4), ("cp_0", "cp_1", "cp_2", "tp_0", "tp_1"))
    placed = (P(CP, TP), P(CP, None), P(CP), P(None, TP), P(None, TP), P(None, TP), P(TP, None))
    return jax.shard_map(
        per_device, mesh=split, in_specs=placed, out_specs=P(CP, TP), check_vma=False
    )
```

profile of v0, /device:TPU:1, one launch (start us, length us, event | category | flops | bytes accessed | tf_op | source)
XLA Modules:
  0.0 774.9 jit_solution(6277096617553391568)
XLA Ops:
  7.3 39.4 %all-gather.2 = s32[16,1,2]{2,1,0:T(1,128)S(1)} all-gather(s32[1,1,2]{2,1,0:T(1,128)} %bitcast.155), channel_id=2, replica_groups=mesh['cp_0'=4,'cp_1'=4,'cp_2'=2,'tp_0'=2,'tp_1'=4] {'cp_0','cp_1'}, dimensions={0}, use_global_device_ids=true | all-gather | bytes 136 | tf_op jit(solution)/shard_map/all_gather | solution.py:24
  46.8 7.9 %all-gather.3 = s32[2,16,2]{1,2,0:T(2,128)S(1)} all-gather(s32[1,16,2]{1,2,0:T(2,128)S(1)} %bitcast.154), channel_id=3, replica_groups=mesh['cp_0'=4,'cp_1'=4,'cp_2'=2,'tp_0'=2,'tp_1'=4] {'cp_2'}, dimensions={0}, use_global_device_ids=true | all-gather | bytes 384 | tf_op jit(solution)/shard_map/all_gather | solution.py:24
  69.2 53.8 %all-gather.6.cloned.1.call-done = bf16[512,4096]{1,0:T(8,128)(2,1)} async-done(((bf16[512,512]{1,0:T(8,128)(2,1)}), bf16[512,4096]{1,0:T(8,128)(2,1)}) %all-gather.6.cloned.1.call-update) | async-done | bytes 4194320 | tf_op jit(solution)/shard_map/all_gather | solution.py:146
  123.0 3.8 convolution_bitcast_fusion
  137.5 3.8 conditional.8
  142.0 3.2 conditional.11
  145.2 510.1 %while.27 = (s32[]{:T(128)}, f32[4,256]{1,0:T(4,128)}, f32[4,256]{1,0:T(4,128)S(1)}, f32[4,256,128]{2,1,0:T(8,128)S(1)}, f32[4,256]{1,0:T(4,128)}, /*index=5*/f3...) while((s32[]{:T(128)}, f32[4,256]{1,0:T(4,128)}, ...), condition=%wide.region_35.36_spmd, body=%wide.region_18.35_spmd.sunk | while | flops 548151296 | bytes 21779492 | solution.py:192
  145.2 3.2 collective-permute-start
  176.5 3.2 conditional.19
  192.4 3.2 conditional.19
  225.9 3.2 conditional.19
  243.2 3.2 conditional.18
  275.9 3.2 conditional.19
  291.9 3.2 conditional.19
  307.9 3.2 conditional.19
  357.3 3.2 conditional.19
  389.3 3.2 conditional.19
  405.3 3.2 conditional.19
  424.0 3.2 conditional.18
  456.0 3.2 conditional.19
  504.0 3.2 conditional.18
  535.9 3.2 conditional.17
  551.9 3.2 conditional.18
  583.8 3.2 conditional.19
  615.7 3.2 conditional.18
  635.5 3.8 collective-permute-start
  655.7 5.1 bitcast_convert_fusion
  660.8 4.2 copy.110
  665.0 6.9 reshape.630
  671.9 5.5 copy.79
  677.5 47.7 %reduce-scatter.3.cloned.1.call-done = bf16[2,512,512]{2,1,0:T(8,128)(2,1)} async-done(((bf16[8,512,512]{2,1,0:T(8,128)(2,1)}), bf16[2,512,512]{2,1,0:T(8,128)(2,1)}) %reduce-scatter.3.cloned.1.call-update) | async-done | bytes 1048592 | tf_op jit(solution)/shard_map/reduce_scatter | solution.py:46
  725.2 43.2 %reduce-scatter.5.cloned.1.call-done = bf16[1,512,512]{2,1,0:T(8,128)(2,1)} async-done(((bf16[2,512,512]{2,1,0:T(8,128)(2,1)}), bf16[1,512,512]{2,1,0:T(8,128)(2,1)}) %reduce-scatter.5.cloned.1.call-update) | async-done | bytes 524304 | tf_op jit(solution)/shard_map/reduce_scatter | solution.py:46
  (653 shorter events, 256.1 us)
Async XLA Ops:
  6.5 116.4 %all-gather.6.cloned.1.call-start = ((), (), s32[]{:S(2)}) async-start(), calls=%async_computation.2 | async-start | bytes 4718592 | tf_op jit(solution)/shard_map/all_gather | solution.py:146
  7.3 717.9 %reduce-scatter.3.cloned.1.call-start = ((), (), s32[]{:S(2)}) async-start(), calls=%async_computation.3 | async-start | bytes 5242880 | tf_op jit(solution)/shard_map/reduce_scatter | solution.py:46
  145.2 15.2 %collective-permute-start = (bf16[2,512,128]{2,1,0:T(8,128)(2,1)}, bf16[2,512,128]{2,1,0:T(8,128)(2,1)S(1)}, u32[]{:S(2)}, u32[]{:S(2)}) collective-permute-start(bf16[2,512,128]{2,1,0:T(8,128)(2,1)} %get-tuple-element.1174), channel_id=1, source_target_pairs={{248,0},{0,8},{8,16},{16,24},{24,32},{32,40},{40,48},{48,56},{56,6... | collective-permute-start | bytes 786440 | tf_op jit(solution)/shard_map/while/body/eval_jaxpr/ppermute | solution.py:38
  164.3 12.0 %collective-permute-start = (bf16[2,512,128]{2,1,0:T(8,128)(2,1)}, bf16[2,512,128]{2,1,0:T(8,128)(2,1)S(1)}, u32[]{:S(2)}, u32[]{:S(2)}) collective-permute-start(bf16[2,512,128]{2,1,0:T(8,128)(2,1)} %get-tuple-element.1174), channel_id=1, source_target_pairs={{248,0},{0,8},{8,16},{16,24},{24,32},{32,40},{40,48},{48,56},{56,6... | collective-permute-start | bytes 786440 | tf_op jit(solution)/shard_map/while/body/eval_jaxpr/ppermute | solution.py:38
  180.3 12.0 %collective-permute-start = (bf16[2,512,128]{2,1,0:T(8,128)(2,1)}, bf16[2,512,128]{2,1,0:T(8,128)(2,1)S(1)}, u32[]{:S(2)}, u32[]{:S(2)}) collective-permute-start(bf16[2,512,128]{2,1,0:T(8,128)(2,1)} %get-tuple-element.1174), channel_id=1, source_target_pairs={{248,0},{0,8},{8,16},{16,24},{24,32},{32,40},{40,48},{48,56},{56,6... | collective-permute-start | bytes 786440 | tf_op jit(solution)/shard_map/while/body/eval_jaxpr/ppermute | solution.py:38
  196.3 13.5 %collective-permute-start = (bf16[2,512,128]{2,1,0:T(8,128)(2,1)}, bf16[2,512,128]{2,1,0:T(8,128)(2,1)S(1)}, u32[]{:S(2)}, u32[]{:S(2)}) collective-permute-start(bf16[2,512,128]{2,1,0:T(8,128)(2,1)} %get-tuple-element.1174), channel_id=1, source_target_pairs={{248,0},{0,8},{8,16},{16,24},{24,32},{32,40},{40,48},{48,56},{56,6... | collective-permute-start | bytes 786440 | tf_op jit(solution)/shard_map/while/body/eval_jaxpr/ppermute | solution.py:38
  213.8 12.0 %collective-permute-start = (bf16[2,512,128]{2,1,0:T(8,128)(2,1)}, bf16[2,512,128]{2,1,0:T(8,128)(2,1)S(1)}, u32[]{:S(2)}, u32[]{:S(2)}) collective-permute-start(bf16[2,512,128]{2,1,0:T(8,128)(2,1)} %get-tuple-element.1174), channel_id=1, source_target_pairs={{248,0},{0,8},{8,16},{16,24},{24,32},{32,40},{40,48},{48,56},{56,6... | collective-permute-start | bytes 786440 | tf_op jit(solution)/shard_map/while/body/eval_jaxpr/ppermute | solution.py:38
  229.7 13.4 %collective-permute-start = (bf16[2,512,128]{2,1,0:T(8,128)(2,1)}, bf16[2,512,128]{2,1,0:T(8,128)(2,1)S(1)}, u32[]{:S(2)}, u32[]{:S(2)}) collective-permute-start(bf16[2,512,128]{2,1,0:T(8,128)(2,1)} %get-tuple-element.1174), channel_id=1, source_target_pairs={{248,0},{0,8},{8,16},{16,24},{24,32},{32,40},{40,48},{48,56},{56,6... | collective-permute-start | bytes 786440 | tf_op jit(solution)/shard_map/while/body/eval_jaxpr/ppermute | solution.py:38
  247.1 12.0 %collective-permute-start = (bf16[2,512,128]{2,1,0:T(8,128)(2,1)}, bf16[2,512,128]{2,1,0:T(8,128)(2,1)S(1)}, u32[]{:S(2)}, u32[]{:S(2)}) collective-permute-start(bf16[2,512,128]{2,1,0:T(8,128)(2,1)} %get-tuple-element.1174), channel_id=1, source_target_pairs={{248,0},{0,8},{8,16},{16,24},{24,32},{32,40},{40,48},{48,56},{56,6... | collective-permute-start | bytes 786440 | tf_op jit(solution)/shard_map/while/body/eval_jaxpr/ppermute | solution.py:38
  263.1 12.7 %collective-permute-start = (bf16[2,512,128]{2,1,0:T(8,128)(2,1)}, bf16[2,512,128]{2,1,0:T(8,128)(2,1)S(1)}, u32[]{:S(2)}, u32[]{:S(2)}) collective-permute-start(bf16[2,512,128]{2,1,0:T(8,128)(2,1)} %get-tuple-element.1174), channel_id=1, source_target_pairs={{248,0},{0,8},{8,16},{16,24},{24,32},{32,40},{40,48},{48,56},{56,6... | collective-permute-start | bytes 786440 | tf_op jit(solution)/shard_map/while/body/eval_jaxpr/ppermute | solution.py:38
  279.8 12.0 %collective-permute-start = (bf16[2,512,128]{2,1,0:T(8,128)(2,1)}, bf16[2,512,128]{2,1,0:T(8,128)(2,1)S(1)}, u32[]{:S(2)}, u32[]{:S(2)}) collective-permute-start(bf16[2,512,128]{2,1,0:T(8,128)(2,1)} %get-tuple-element.1174), channel_id=1, source_target_pairs={{248,0},{0,8},{8,16},{16,24},{24,32},{32,40},{40,48},{48,56},{56,6... | collective-permute-start | bytes 786440 | tf_op jit(solution)/shard_map/while/body/eval_jaxpr/ppermute | solution.py:38
  295.8 12.0 %collective-permute-start = (bf16[2,512,128]{2,1,0:T(8,128)(2,1)}, bf16[2,512,128]{2,1,0:T(8,128)(2,1)S(1)}, u32[]{:S(2)}, u32[]{:S(2)}) collective-permute-start(bf16[2,512,128]{2,1,0:T(8,128)(2,1)} %get-tuple-element.1174), channel_id=1, source_target_pairs={{248,0},{0,8},{8,16},{16,24},{24,32},{32,40},{40,48},{48,56},{56,6... | collective-permute-start | bytes 786440 | tf_op jit(solution)/shard_map/while/body/eval_jaxpr/ppermute | solution.py:38
  311.8 13.4 %collective-permute-start = (bf16[2,512,128]{2,1,0:T(8,128)(2,1)}, bf16[2,512,128]{2,1,0:T(8,128)(2,1)S(1)}, u32[]{:S(2)}, u32[]{:S(2)}) collective-permute-start(bf16[2,512,128]{2,1,0:T(8,128)(2,1)} %get-tuple-element.1174), channel_id=1, source_target_pairs={{248,0},{0,8},{8,16},{16,24},{24,32},{32,40},{40,48},{48,56},{56,6... | collective-permute-start | bytes 786440 | tf_op jit(solution)/shard_map/while/body/eval_jaxpr/ppermute | solution.py:38
  329.1 12.1 %collective-permute-start = (bf16[2,512,128]{2,1,0:T(8,128)(2,1)}, bf16[2,512,128]{2,1,0:T(8,128)(2,1)S(1)}, u32[]{:S(2)}, u32[]{:S(2)}) collective-permute-start(bf16[2,512,128]{2,1,0:T(8,128)(2,1)} %get-tuple-element.1174), channel_id=1, source_target_pairs={{248,0},{0,8},{8,16},{16,24},{24,32},{32,40},{40,48},{48,56},{56,6... | collective-permute-start | bytes 786440 | tf_op jit(solution)/shard_map/while/body/eval_jaxpr/ppermute | solution.py:38
  345.2 12.0 %collective-permute-start = (bf16[2,512,128]{2,1,0:T(8,128)(2,1)}, bf16[2,512,128]{2,1,0:T(8,128)(2,1)S(1)}, u32[]{:S(2)}, u32[]{:S(2)}) collective-permute-start(bf16[2,512,128]{2,1,0:T(8,128)(2,1)} %get-tuple-element.1174), channel_id=1, source_target_pairs={{248,0},{0,8},{8,16},{16,24},{24,32},{32,40},{40,48},{48,56},{56,6... | collective-permute-start | bytes 786440 | tf_op jit(solution)/shard_map/while/body/eval_jaxpr/ppermute | solution.py:38
  361.2 12.0 %collective-permute-start = (bf16[2,512,128]{2,1,0:T(8,128)(2,1)}, bf16[2,512,128]{2,1,0:T(8,128)(2,1)S(1)}, u32[]{:S(2)}, u32[]{:S(2)}) collective-permute-start(bf16[2,512,128]{2,1,0:T(8,128)(2,1)} %get-tuple-element.1174), channel_id=1, source_target_pairs={{248,0},{0,8},{8,16},{16,24},{24,32},{32,40},{40,48},{48,56},{56,6... | collective-permute-start | bytes 786440 | tf_op jit(solution)/shard_map/while/body/eval_jaxpr/ppermute | solution.py:38
  377.2 12.0 %collective-permute-start = (bf16[2,512,128]{2,1,0:T(8,128)(2,1)}, bf16[2,512,128]{2,1,0:T(8,128)(2,1)S(1)}, u32[]{:S(2)}, u32[]{:S(2)}) collective-permute-start(bf16[2,512,128]{2,1,0:T(8,128)(2,1)} %get-tuple-element.1174), channel_id=1, source_target_pairs={{248,0},{0,8},{8,16},{16,24},{24,32},{32,40},{40,48},{48,56},{56,6... | collective-permute-start | bytes 786440 | tf_op jit(solution)/shard_map/while/body/eval_jaxpr/ppermute | solution.py:38
  393.2 12.0 %collective-permute-start = (bf16[2,512,128]{2,1,0:T(8,128)(2,1)}, bf16[2,512,128]{2,1,0:T(8,128)(2,1)S(1)}, u32[]{:S(2)}, u32[]{:S(2)}) collective-permute-start(bf16[2,512,128]{2,1,0:T(8,128)(2,1)} %get-tuple-element.1174), channel_id=1, source_target_pairs={{248,0},{0,8},{8,16},{16,24},{24,32},{32,40},{40,48},{48,56},{56,6... | collective-permute-start | bytes 786440 | tf_op jit(solution)/shard_map/while/body/eval_jaxpr/ppermute | solution.py:38
  409.1 14.8 %collective-permute-start = (bf16[2,512,128]{2,1,0:T(8,128)(2,1)}, bf16[2,512,128]{2,1,0:T(8,128)(2,1)S(1)}, u32[]{:S(2)}, u32[]{:S(2)}) collective-permute-start(bf16[2,512,128]{2,1,0:T(8,128)(2,1)} %get-tuple-element.1174), channel_id=1, source_target_pairs={{248,0},{0,8},{8,16},{16,24},{24,32},{32,40},{40,48},{48,56},{56,6... | collective-permute-start | bytes 786440 | tf_op jit(solution)/shard_map/while/body/eval_jaxpr/ppermute | solution.py:38
  427.9 12.0 %collective-permute-start = (bf16[2,512,128]{2,1,0:T(8,128)(2,1)}, bf16[2,512,128]{2,1,0:T(8,128)(2,1)S(1)}, u32[]{:S(2)}, u32[]{:S(2)}) collective-permute-start(bf16[2,512,128]{2,1,0:T(8,128)(2,1)} %get-tuple-element.1174), channel_id=1, source_target_pairs={{248,0},{0,8},{8,16},{16,24},{24,32},{32,40},{40,48},{48,56},{56,6... | collective-permute-start | bytes 786440 | tf_op jit(solution)/shard_map/while/body/eval_jaxpr/ppermute | solution.py:38
  443.9 12.1 %collective-permute-start = (bf16[2,512,128]{2,1,0:T(8,128)(2,1)}, bf16[2,512,128]{2,1,0:T(8,128)(2,1)S(1)}, u32[]{:S(2)}, u32[]{:S(2)}) collective-permute-start(bf16[2,512,128]{2,1,0:T(8,128)(2,1)} %get-tuple-element.1174), channel_id=1, source_target_pairs={{248,0},{0,8},{8,16},{16,24},{24,32},{32,40},{40,48},{48,56},{56,6... | collective-permute-start | bytes 786440 | tf_op jit(solution)/shard_map/while/body/eval_jaxpr/ppermute | solution.py:38
  459.9 12.0 %collective-permute-start = (bf16[2,512,128]{2,1,0:T(8,128)(2,1)}, bf16[2,512,128]{2,1,0:T(8,128)(2,1)S(1)}, u32[]{:S(2)}, u32[]{:S(2)}) collective-permute-start(bf16[2,512,128]{2,1,0:T(8,128)(2,1)} %get-tuple-element.1174), channel_id=1, source_target_pairs={{248,0},{0,8},{8,16},{16,24},{24,32},{32,40},{40,48},{48,56},{56,6... | collective-permute-start | bytes 786440 | tf_op jit(solution)/shard_map/while/body/eval_jaxpr/ppermute | solution.py:38
  475.9 12.0 %collective-permute-start = (bf16[2,512,128]{2,1,0:T(8,128)(2,1)}, bf16[2,512,128]{2,1,0:T(8,128)(2,1)S(1)}, u32[]{:S(2)}, u32[]{:S(2)}) collective-permute-start(bf16[2,512,128]{2,1,0:T(8,128)(2,1)} %get-tuple-element.1174), channel_id=1, source_target_pairs={{248,0},{0,8},{8,16},{16,24},{24,32},{32,40},{40,48},{48,56},{56,6... | collective-permute-start | bytes 786440 | tf_op jit(solution)/shard_map/while/body/eval_jaxpr/ppermute | solution.py:38
  491.9 12.0 %collective-permute-start = (bf16[2,512,128]{2,1,0:T(8,128)(2,1)}, bf16[2,512,128]{2,1,0:T(8,128)(2,1)S(1)}, u32[]{:S(2)}, u32[]{:S(2)}) collective-permute-start(bf16[2,512,128]{2,1,0:T(8,128)(2,1)} %get-tuple-element.1174), channel_id=1, source_target_pairs={{248,0},{0,8},{8,16},{16,24},{24,32},{32,40},{40,48},{48,56},{56,6... | collective-permute-start | bytes 786440 | tf_op jit(solution)/shard_map/while/body/eval_jaxpr/ppermute | solution.py:38
  507.8 12.0 %collective-permute-start = (bf16[2,512,128]{2,1,0:T(8,128)(2,1)}, bf16[2,512,128]{2,1,0:T(8,128)(2,1)S(1)}, u32[]{:S(2)}, u32[]{:S(2)}) collective-permute-start(bf16[2,512,128]{2,1,0:T(8,128)(2,1)} %get-tuple-element.1174), channel_id=1, source_target_pairs={{248,0},{0,8},{8,16},{16,24},{24,32},{32,40},{40,48},{48,56},{56,6... | collective-permute-start | bytes 786440 | tf_op jit(solution)/shard_map/while/body/eval_jaxpr/ppermute | solution.py:38
  523.8 12.0 %collective-permute-start = (bf16[2,512,128]{2,1,0:T(8,128)(2,1)}, bf16[2,512,128]{2,1,0:T(8,128)(2,1)S(1)}, u32[]{:S(2)}, u32[]{:S(2)}) collective-permute-start(bf16[2,512,128]{2,1,0:T(8,128)(2,1)} %get-tuple-element.1174), channel_id=1, source_target_pairs={{248,0},{0,8},{8,16},{16,24},{24,32},{32,40},{40,48},{48,56},{56,6... | collective-permute-start | bytes 786440 | tf_op jit(solution)/shard_map/while/body/eval_jaxpr/ppermute | solution.py:38
  539.8 12.0 %collective-permute-start = (bf16[2,512,128]{2,1,0:T(8,128)(2,1)}, bf16[2,512,128]{2,1,0:T(8,128)(2,1)S(1)}, u32[]{:S(2)}, u32[]{:S(2)}) collective-permute-start(bf16[2,512,128]{2,1,0:T(8,128)(2,1)} %get-tuple-element.1174), channel_id=1, source_target_pairs={{248,0},{0,8},{8,16},{16,24},{24,32},{32,40},{40,48},{48,56},{56,6... | collective-permute-start | bytes 786440 | tf_op jit(solution)/shard_map/while/body/eval_jaxpr/ppermute | solution.py:38
  555.8 12.0 %collective-permute-start = (bf16[2,512,128]{2,1,0:T(8,128)(2,1)}, bf16[2,512,128]{2,1,0:T(8,128)(2,1)S(1)}, u32[]{:S(2)}, u32[]{:S(2)}) collective-permute-start(bf16[2,512,128]{2,1,0:T(8,128)(2,1)} %get-tuple-element.1174), channel_id=1, source_target_pairs={{248,0},{0,8},{8,16},{16,24},{24,32},{32,40},{40,48},{48,56},{56,6... | collective-permute-start | bytes 786440 | tf_op jit(solution)/shard_map/while/body/eval_jaxpr/ppermute | solution.py:38
  571.7 12.0 %collective-permute-start = (bf16[2,512,128]{2,1,0:T(8,128)(2,1)}, bf16[2,512,128]{2,1,0:T(8,128)(2,1)S(1)}, u32[]{:S(2)}, u32[]{:S(2)}) collective-permute-start(bf16[2,512,128]{2,1,0:T(8,128)(2,1)} %get-tuple-element.1174), channel_id=1, source_target_pairs={{248,0},{0,8},{8,16},{16,24},{24,32},{32,40},{40,48},{48,56},{56,6... | collective-permute-start | bytes 786440 | tf_op jit(solution)/shard_map/while/body/eval_jaxpr/ppermute | solution.py:38
  600.5 15.1 %collective-permute-start = (bf16[2,512,128]{2,1,0:T(8,128)(2,1)}, bf16[2,512,128]{2,1,0:T(8,128)(2,1)S(1)}, u32[]{:S(2)}, u32[]{:S(2)}) collective-permute-start(bf16[2,512,128]{2,1,0:T(8,128)(2,1)} %get-tuple-element.1174), channel_id=1, source_target_pairs={{248,0},{0,8},{8,16},{16,24},{24,32},{32,40},{40,48},{48,56},{56,6... | collective-permute-start | bytes 786440 | tf_op jit(solution)/shard_map/while/body/eval_jaxpr/ppermute | solution.py:38
  635.5 15.8 %collective-permute-start = (bf16[2,512,128]{2,1,0:T(8,128)(2,1)}, bf16[2,512,128]{2,1,0:T(8,128)(2,1)S(1)}, u32[]{:S(2)}, u32[]{:S(2)}) collective-permute-start(bf16[2,512,128]{2,1,0:T(8,128)(2,1)} %get-tuple-element.1174), channel_id=1, source_target_pairs={{248,0},{0,8},{8,16},{16,24},{24,32},{32,40},{40,48},{48,56},{56,6... | collective-permute-start | bytes 786440 | tf_op jit(solution)/shard_map/while/body/eval_jaxpr/ppermute | solution.py:38
  677.4 91.0 %reduce-scatter.5.cloned.1.call-start = ((), (), s32[]{:S(2)}) async-start(), calls=%async_computation.4 | async-start | bytes 1572864 | tf_op jit(solution)/shard_map/reduce_scatter | solution.py:46
  (6 other events, 206.7 us)
Sparse Core Ops, SparseCore 0:
  9.8 113.1 all-gather.5
  677.5 47.6 reduce-scatter.2
  727.7 40.6 reduce-scatter.4
where the time goes:
time: 782 us; the launch traced here: 775 us
  loops' own time  314 us (40%)
  waiting for transfers between devices  146 us (19%)
  local copies, waits for them, and re-layouts  124 us (16%)
  other arithmetic  62.2 us (8%)
  blocking collectives  47.4 us (6%)
  matrix products  40.1 us (5%)
  between operations  23.4 us (3%)
  starting transfers between devices  18.2 us (2%)
    another operation x1, loops' own time, per_device(): lax.fori_loop(0, rank_count - 1, turn, (halves, jnp.stack((keys_here, val...  311 us
    reduce_scatter x2, waiting for transfers between devices, sum_in_order(): pieces = lax.psum_scatter(pieces, axes[k], scatter_dimension=0, tiled=True)  90.9 us
    all_gather x1, waiting for transfers between devices, per_device(): pieces = lax.all_gather(tokens, TP, axis=1, tiled=True)  53.8 us
    all_gather x2, blocking collectives, all_blocks(): pieces = lax.all_gather(pieces, axes[k], axis=0, tiled=True)  47.4 us
    slice x62, local copies, waits for them, and re-layouts, attend(): query_index[-1]  38.8 us
    add x32, other arithmetic, block_update(): weight_sum = weight_sum * rescale + jnp.sum(weights, axis=-1)  22.2 us
    while x31, local copies, waits for them, and re-layouts  21.6 us
    max x31, other arithmetic, block_update(): new_max = jnp.maximum(row_max, jnp.max(scores, axis=-1))  21.2 us
  transfers between devices with their start and end apart: 34, of which 3 were waited for; matrix products, arithmetic and copies ran while one was open for 9% of the time, Pallas kernels for 0%

commit v1 on v0

--- a/solution.py
+++ b/solution.py
@@ -143,7 +143,9 @@
     half_rows = row_count // 2
     head_count = q_weight.shape[1] // HD
     weights_in = (q_weight, k_weight, v_weight)
-    pieces = lax.all_gather(tokens, TP, axis=1, tiled=True)
+    pieces = jnp.concatenate(
+        lax.all_to_all(jnp.stack(lax.axis_size(TP) * [tokens]), TP, split_axis=0, concat_axis=0), 1
+    )
     queries, keys_here, values_here = tuple(
         (jnp.dot(pieces, matrix, preferred_element_type=jnp.float32) for matrix in weights_in)
     )

time: 782 us -> 827 us (1.058)
  blocking collectives: 47.4 us -> 121 us
  waiting for transfers between devices: 146 us -> 99.8 us
  starting transfers between devices: 18.2 us -> 29.8 us
    all_gather x2, blocking collectives: 47.4 us -> 121 us  [all_blocks(): pieces = lax.all_gather(pieces, axes[k], axis=0, tiled=True)]
    all_gather x1 -> x0, waiting for transfers between devices: 53.8 us -> none  [per_device(): pieces = lax.all_gather(tokens, TP, axis=1, tiled=True)]
    while x31, local copies, waits for them, and re-layouts: 21.6 us -> 0.56 us
    reshape x0 -> x3, local copies, waits for them, and re-layouts: none -> 16.7 us  [per_device(): jnp.concatenate(lax.all_to_all(jnp.stack(lax.axis_size(TP) * [tokens]), T...]
    all_to_all x0 -> x1, starting transfers between devices: none -> 11.6 us  [per_device(): lax.all_to_all(jnp.stack(lax.axis_size(TP) * [tokens]), TP, split_axis=0,...]
    reduce_scatter x2, waiting for transfers between devices: 90.9 us -> 99.7 us  [sum_in_order(): pieces = lax.psum_scatter(pieces, axes[k], scatter_dimension=0, tiled=True)]
  transfers between devices with their start and end apart: 34 -> 34, of which waited for: 3 -> 2; matrix products, arithmetic and copies ran while one was open for 9% -> 9% of each run, Pallas kernels for 0% -> 0%
where the time goes in v1:
time: 827 us; the launch traced here: 820 us
  loops' own time  317 us (38%)
  local copies, waits for them, and re-layouts  128 us (15%)
  blocking collectives  121 us (15%)
  waiting for transfers between devices  99.8 us (12%)
  other arithmetic  57.9 us (7%)
  matrix products  43.4 us (5%)
  starting transfers between devices  29.8 us (4%)
  between operations  23.3 us (3%)
    another operation x1, loops' own time, per_device(): lax.fori_loop(0, rank_count - 1, turn, (halves, jnp.stack((keys_here, val...  314 us
    all_gather x2, blocking collectives, all_blocks(): pieces = lax.all_gather(pieces, axes[k], axis=0, tiled=True)  121 us
    reduce_scatter x2, waiting for transfers between devices, sum_in_order(): pieces = lax.psum_scatter(pieces, axes[k], scatter_dimension=0, tiled=True)  99.7 us
    slice x62, local copies, waits for them, and re-layouts, attend(): query_index[-1]  39.7 us
    add x32, other arithmetic, block_update(): weight_sum = weight_sum * rescale + jnp.sum(weights, axis=-1)  22.2 us
    max x31, other arithmetic, block_update(): new_max = jnp.maximum(row_max, jnp.max(scores, axis=-1))  21.3 us
    slice x31, local copies, waits for them, and re-layouts, attend(): index_rows[-1] >= lowest_start  20.8 us
    cond x31, local copies, waits for them, and re-layouts  18.4 us
  transfers between devices with their start and end apart: 34, of which 2 were waited for; matrix products, arithmetic and copies ran while one was open for 9% of the time, Pallas kernels for 0%

profile of v1, /device:TPU:1, one launch (start us, length us, event | category | flops | bytes accessed | tf_op | source)
XLA Modules:
  0.0 819.6 jit_solution(2408055725715267972)
XLA Ops:
  6.5 3.5 stack.6
  10.0 11.6 %all-to-all-start = ((bf16[8,512,512]{2,1,0:T(8,128)(2,1)}), bf16[8,512,512]{2,1,0:T(8,128)(2,1)}, u32[]{:S(2)}, u32[]{:S(2)}) async-start(bf16[8,512,512]{2,1,0:T(8,128)(2,1)} %stack.6), calls=%async_computation | async-start | bytes 8388608 | tf_op jit(solution)/shard_map/all_to_all | solution.py:147
  21.7 112.3 %all-gather.2 = s32[16,1,2]{2,1,0:T(1,128)S(1)} all-gather(s32[1,1,2]{2,1,0:T(1,128)S(1)} %bitcast.162), channel_id=2, replica_groups=mesh['cp_0'=4,'cp_1'=4,'cp_2'=2,'tp_0'=2,'tp_1'=4] {'cp_0','cp_1'}, dimensions={0}, use_global_device_ids=true | all-gather | bytes 136 | tf_op jit(solution)/shard_map/all_gather | solution.py:24
  134.0 8.5 %all-gather.3 = s32[2,16,2]{1,2,0:T(2,128)S(1)} all-gather(s32[1,16,2]{1,2,0:T(2,128)S(1)} %bitcast.161), channel_id=3, replica_groups=mesh['cp_0'=4,'cp_1'=4,'cp_2'=2,'tp_0'=2,'tp_1'=4] {'cp_2'}, dimensions={0}, use_global_device_ids=true | all-gather | bytes 384 | tf_op jit(solution)/shard_map/all_gather | solution.py:24
  153.8 6.4 copy.126
  165.7 6.5 copy.77
  172.2 7.5 reshape.669
  179.6 3.7 convolution_convert_fusion
  183.6 5.8 fusion.108
  190.0 3.8 conditional.8
  194.5 3.2 conditional.11
  197.7 493.0 %while.27 = (s32[]{:T(128)}, f32[4,256]{1,0:T(4,128)}, f32[4,256]{1,0:T(4,128)S(1)}, f32[4,256,128]{2,1,0:T(8,128)S(1)}, f32[4,256]{1,0:T(4,128)}, /*index=5*/f3...) while((s32[]{:T(128)}, f32[4,256]{1,0:T(4,128)}, ...), condition=%wide.region_35.36_spmd, body=%wide.region_18.35_spmd.sunk | while | flops 548151296 | bytes 21779492 | solution.py:194
  226.1 3.2 conditional.19
  335.9 3.2 conditional.19
  351.4 3.2 conditional.19
  368.2 3.2 conditional.18
  478.1 3.2 conditional.18
  555.7 3.2 conditional.19
  571.2 3.2 conditional.17
  586.8 3.2 conditional.18
  602.3 3.2 conditional.18
  633.4 6.2 collective-permute-start
  651.8 3.2 conditional.18
  667.3 3.2 conditional.19
  670.5 4.8 collective-permute-start
  687.5 3.2 conditional.19
  691.1 5.1 bitcast_convert_fusion
  696.2 4.2 copy.130
  700.4 6.9 reshape.638
  707.3 5.6 copy.95
  713.0 56.6 %reduce-scatter.3.cloned.1.call-done = bf16[2,512,512]{2,1,0:T(8,128)(2,1)} async-done(((bf16[8,512,512]{2,1,0:T(8,128)(2,1)}), bf16[2,512,512]{2,1,0:T(8,128)(2,1)}) %reduce-scatter.3.cloned.1.call-update) | async-done | bytes 1048592 | tf_op jit(solution)/shard_map/reduce_scatter | solution.py:46
  769.6 43.2 %reduce-scatter.5.cloned.1.call-done = bf16[1,512,512]{2,1,0:T(8,128)(2,1)} async-done(((bf16[2,512,512]{2,1,0:T(8,128)(2,1)}), bf16[1,512,512]{2,1,0:T(8,128)(2,1)}) %reduce-scatter.5.cloned.1.call-update) | async-done | bytes 524304 | tf_op jit(solution)/shard_map/reduce_scatter | solution.py:46
  (660 shorter events, 240.6 us)
Async XLA Ops:
  10.0 150.7 %all-to-all-start = ((bf16[8,512,512]{2,1,0:T(8,128)(2,1)}), bf16[8,512,512]{2,1,0:T(8,128)(2,1)}, u32[]{:S(2)}, u32[]{:S(2)}) async-start(bf16[8,512,512]{2,1,0:T(8,128)(2,1)} %stack.6), calls=%async_computation | async-start | bytes 8388608 | tf_op jit(solution)/shard_map/all_to_all | solution.py:147
  21.6 748.0 %reduce-scatter.3.cloned.1.call-start = ((), (), s32[]{:S(2)}) async-start(), calls=%async_computation.3 | async-start | bytes 5242880 | tf_op jit(solution)/shard_map/reduce_scatter | solution.py:46
  197.7 12.8 %collective-permute-start = (bf16[2,512,128]{2,1,0:T(8,128)(2,1)S(1)}, bf16[2,512,128]{2,1,0:T(8,128)(2,1)S(1)}, u32[]{:S(2)}, u32[]{:S(2)}) collective-permute-start(bf16[2,512,128]{2,1,0:T(8,128)(2,1)S(1)} %get-tuple-element.1172), channel_id=1, source_target_pairs={{248,0},{0,8},{8,16},{16,24},{24,32},{32,40},{40,48},{48,56},{56,6... | collective-permute-start | bytes 786440 | tf_op jit(solution)/shard_map/while/body/eval_jaxpr/ppermute | solution.py:38
  213.8 12.2 %collective-permute-start = (bf16[2,512,128]{2,1,0:T(8,128)(2,1)S(1)}, bf16[2,512,128]{2,1,0:T(8,128)(2,1)S(1)}, u32[]{:S(2)}, u32[]{:S(2)}) collective-permute-start(bf16[2,512,128]{2,1,0:T(8,128)(2,1)S(1)} %get-tuple-element.1172), channel_id=1, source_target_pairs={{248,0},{0,8},{8,16},{16,24},{24,32},{32,40},{40,48},{48,56},{56,6... | collective-permute-start | bytes 786440 | tf_op jit(solution)/shard_map/while/body/eval_jaxpr/ppermute | solution.py:38
  229.3 12.2 %collective-permute-start = (bf16[2,512,128]{2,1,0:T(8,128)(2,1)S(1)}, bf16[2,512,128]{2,1,0:T(8,128)(2,1)S(1)}, u32[]{:S(2)}, u32[]{:S(2)}) collective-permute-start(bf16[2,512,128]{2,1,0:T(8,128)(2,1)S(1)} %get-tuple-element.1172), channel_id=1, source_target_pairs={{248,0},{0,8},{8,16},{16,24},{24,32},{32,40},{40,48},{48,56},{56,6... | collective-permute-start | bytes 786440 | tf_op jit(solution)/shard_map/while/body/eval_jaxpr/ppermute | solution.py:38
  244.9 12.2 %collective-permute-start = (bf16[2,512,128]{2,1,0:T(8,128)(2,1)S(1)}, bf16[2,512,128]{2,1,0:T(8,128)(2,1)S(1)}, u32[]{:S(2)}, u32[]{:S(2)}) collective-permute-start(bf16[2,512,128]{2,1,0:T(8,128)(2,1)S(1)} %get-tuple-element.1172), channel_id=1, source_target_pairs={{248,0},{0,8},{8,16},{16,24},{24,32},{32,40},{40,48},{48,56},{56,6... | collective-permute-start | bytes 786440 | tf_op jit(solution)/shard_map/while/body/eval_jaxpr/ppermute | solution.py:38
  260.4 12.2 %collective-permute-start = (bf16[2,512,128]{2,1,0:T(8,128)(2,1)S(1)}, bf16[2,512,128]{2,1,0:T(8,128)(2,1)S(1)}, u32[]{:S(2)}, u32[]{:S(2)}) collective-permute-start(bf16[2,512,128]{2,1,0:T(8,128)(2,1)S(1)} %get-tuple-element.1172), channel_id=1, source_target_pairs={{248,0},{0,8},{8,16},{16,24},{24,32},{32,40},{40,48},{48,56},{56,6... | collective-permute-start | bytes 786440 | tf_op jit(solution)/shard_map/while/body/eval_jaxpr/ppermute | solution.py:38
  275.9 12.2 %collective-permute-start = (bf16[2,512,128]{2,1,0:T(8,128)(2,1)S(1)}, bf16[2,512,128]{2,1,0:T(8,128)(2,1)S(1)}, u32[]{:S(2)}, u32[]{:S(2)}) collective-permute-start(bf16[2,512,128]{2,1,0:T(8,128)(2,1)S(1)} %get-tuple-element.1172), channel_id=1, source_target_pairs={{248,0},{0,8},{8,16},{16,24},{24,32},{32,40},{40,48},{48,56},{56,6... | collective-permute-start | bytes 786440 | tf_op jit(solution)/shard_map/while/body/eval_jaxpr/ppermute | solution.py:38
  291.5 12.2 %collective-permute-start = (bf16[2,512,128]{2,1,0:T(8,128)(2,1)S(1)}, bf16[2,512,128]{2,1,0:T(8,128)(2,1)S(1)}, u32[]{:S(2)}, u32[]{:S(2)}) collective-permute-start(bf16[2,512,128]{2,1,0:T(8,128)(2,1)S(1)} %get-tuple-element.1172), channel_id=1, source_target_pairs={{248,0},{0,8},{8,16},{16,24},{24,32},{32,40},{40,48},{48,56},{56,6... | collective-permute-start | bytes 786440 | tf_op jit(solution)/shard_map/while/body/eval_jaxpr/ppermute | solution.py:38
  307.0 13.2 %collective-permute-start = (bf16[2,512,128]{2,1,0:T(8,128)(2,1)S(1)}, bf16[2,512,128]{2,1,0:T(8,128)(2,1)S(1)}, u32[]{:S(2)}, u32[]{:S(2)}) collective-permute-start(bf16[2,512,128]{2,1,0:T(8,128)(2,1)S(1)} %get-tuple-element.1172), channel_id=1, source_target_pairs={{248,0},{0,8},{8,16},{16,24},{24,32},{32,40},{40,48},{48,56},{56,6... | collective-permute-start | bytes 786440 | tf_op jit(solution)/shard_map/while/body/eval_jaxpr/ppermute | solution.py:38
  323.5 12.2 %collective-permute-start = (bf16[2,512,128]{2,1,0:T(8,128)(2,1)S(1)}, bf16[2,512,128]{2,1,0:T(8,128)(2,1)S(1)}, u32[]{:S(2)}, u32[]{:S(2)}) collective-permute-start(bf16[2,512,128]{2,1,0:T(8,128)(2,1)S(1)} %get-tuple-element.1172), channel_id=1, source_target_pairs={{248,0},{0,8},{8,16},{16,24},{24,32},{32,40},{40,48},{48,56},{56,6... | collective-permute-start | bytes 786440 | tf_op jit(solution)/shard_map/while/body/eval_jaxpr/ppermute | solution.py:38
  339.1 12.2 %collective-permute-start = (bf16[2,512,128]{2,1,0:T(8,128)(2,1)S(1)}, bf16[2,512,128]{2,1,0:T(8,128)(2,1)S(1)}, u32[]{:S(2)}, u32[]{:S(2)}) collective-permute-start(bf16[2,512,128]{2,1,0:T(8,128)(2,1)S(1)} %get-tuple-element.1172), channel_id=1, source_target_pairs={{248,0},{0,8},{8,16},{16,24},{24,32},{32,40},{40,48},{48,56},{56,6... | collective-permute-start | bytes 786440 | tf_op jit(solution)/shard_map/while/body/eval_jaxpr/ppermute | solution.py:38
  354.6 13.6 %collective-permute-start = (bf16[2,512,128]{2,1,0:T(8,128)(2,1)S(1)}, bf16[2,512,128]{2,1,0:T(8,128)(2,1)S(1)}, u32[]{:S(2)}, u32[]{:S(2)}) collective-permute-start(bf16[2,512,128]{2,1,0:T(8,128)(2,1)S(1)} %get-tuple-element.1172), channel_id=1, source_target_pairs={{248,0},{0,8},{8,16},{16,24},{24,32},{32,40},{40,48},{48,56},{56,6... | collective-permute-start | bytes 786440 | tf_op jit(solution)/shard_map/while/body/eval_jaxpr/ppermute | solution.py:38
  371.4 12.3 %collective-permute-start = (bf16[2,512,128]{2,1,0:T(8,128)(2,1)S(1)}, bf16[2,512,128]{2,1,0:T(8,128)(2,1)S(1)}, u32[]{:S(2)}, u32[]{:S(2)}) collective-permute-start(bf16[2,512,128]{2,1,0:T(8,128)(2,1)S(1)} %get-tuple-element.1172), channel_id=1, source_target_pairs={{248,0},{0,8},{8,16},{16,24},{24,32},{32,40},{40,48},{48,56},{56,6... | collective-permute-start | bytes 786440 | tf_op jit(solution)/shard_map/while/body/eval_jaxpr/ppermute | solution.py:38
  387.0 12.2 %collective-permute-start = (bf16[2,512,128]{2,1,0:T(8,128)(2,1)S(1)}, bf16[2,512,128]{2,1,0:T(8,128)(2,1)S(1)}, u32[]{:S(2)}, u32[]{:S(2)}) collective-permute-start(bf16[2,512,128]{2,1,0:T(8,128)(2,1)S(1)} %get-tuple-element.1172), channel_id=1, source_target_pairs={{248,0},{0,8},{8,16},{16,24},{24,32},{32,40},{40,48},{48,56},{56,6... | collective-permute-start | bytes 786440 | tf_op jit(solution)/shard_map/while/body/eval_jaxpr/ppermute | solution.py:38
  402.6 12.2 %collective-permute-start = (bf16[2,512,128]{2,1,0:T(8,128)(2,1)S(1)}, bf16[2,512,128]{2,1,0:T(8,128)(2,1)S(1)}, u32[]{:S(2)}, u32[]{:S(2)}) collective-permute-start(bf16[2,512,128]{2,1,0:T(8,128)(2,1)S(1)} %get-tuple-element.1172), channel_id=1, source_target_pairs={{248,0},{0,8},{8,16},{16,24},{24,32},{32,40},{40,48},{48,56},{56,6... | collective-permute-start | bytes 786440 | tf_op jit(solution)/shard_map/while/body/eval_jaxpr/ppermute | solution.py:38
  418.1 12.2 %collective-permute-start = (bf16[2,512,128]{2,1,0:T(8,128)(2,1)S(1)}, bf16[2,512,128]{2,1,0:T(8,128)(2,1)S(1)}, u32[]{:S(2)}, u32[]{:S(2)}) collective-permute-start(bf16[2,512,128]{2,1,0:T(8,128)(2,1)S(1)} %get-tuple-element.1172), channel_id=1, source_target_pairs={{248,0},{0,8},{8,16},{16,24},{24,32},{32,40},{40,48},{48,56},{56,6... | collective-permute-start | bytes 786440 | tf_op jit(solution)/shard_map/while/body/eval_jaxpr/ppermute | solution.py:38
  433.6 12.2 %collective-permute-start = (bf16[2,512,128]{2,1,0:T(8,128)(2,1)S(1)}, bf16[2,512,128]{2,1,0:T(8,128)(2,1)S(1)}, u32[]{:S(2)}, u32[]{:S(2)}) collective-permute-start(bf16[2,512,128]{2,1,0:T(8,128)(2,1)S(1)} %get-tuple-element.1172), channel_id=1, source_target_pairs={{248,0},{0,8},{8,16},{16,24},{24,32},{32,40},{40,48},{48,56},{56,6... | collective-permute-start | bytes 786440 | tf_op jit(solution)/shard_map/while/body/eval_jaxpr/ppermute | solution.py:38
  449.1 13.3 %collective-permute-start = (bf16[2,512,128]{2,1,0:T(8,128)(2,1)S(1)}, bf16[2,512,128]{2,1,0:T(8,128)(2,1)S(1)}, u32[]{:S(2)}, u32[]{:S(2)}) collective-permute-start(bf16[2,512,128]{2,1,0:T(8,128)(2,1)S(1)} %get-tuple-element.1172), channel_id=1, source_target_pairs={{248,0},{0,8},{8,16},{16,24},{24,32},{32,40},{40,48},{48,56},{56,6... | collective-permute-start | bytes 786440 | tf_op jit(solution)/shard_map/while/body/eval_jaxpr/ppermute | solution.py:38
  465.8 12.2 %collective-permute-start = (bf16[2,512,128]{2,1,0:T(8,128)(2,1)S(1)}, bf16[2,512,128]{2,1,0:T(8,128)(2,1)S(1)}, u32[]{:S(2)}, u32[]{:S(2)}) collective-permute-start(bf16[2,512,128]{2,1,0:T(8,128)(2,1)S(1)} %get-tuple-element.1172), channel_id=1, source_target_pairs={{248,0},{0,8},{8,16},{16,24},{24,32},{32,40},{40,48},{48,56},{56,6... | collective-permute-start | bytes 786440 | tf_op jit(solution)/shard_map/while/body/eval_jaxpr/ppermute | solution.py:38
  481.3 12.3 %collective-permute-start = (bf16[2,512,128]{2,1,0:T(8,128)(2,1)S(1)}, bf16[2,512,128]{2,1,0:T(8,128)(2,1)S(1)}, u32[]{:S(2)}, u32[]{:S(2)}) collective-permute-start(bf16[2,512,128]{2,1,0:T(8,128)(2,1)S(1)} %get-tuple-element.1172), channel_id=1, source_target_pairs={{248,0},{0,8},{8,16},{16,24},{24,32},{32,40},{40,48},{48,56},{56,6... | collective-permute-start | bytes 786440 | tf_op jit(solution)/shard_map/while/body/eval_jaxpr/ppermute | solution.py:38
  496.9 12.2 %collective-permute-start = (bf16[2,512,128]{2,1,0:T(8,128)(2,1)S(1)}, bf16[2,512,128]{2,1,0:T(8,128)(2,1)S(1)}, u32[]{:S(2)}, u32[]{:S(2)}) collective-permute-start(bf16[2,512,128]{2,1,0:T(8,128)(2,1)S(1)} %get-tuple-element.1172), channel_id=1, source_target_pairs={{248,0},{0,8},{8,16},{16,24},{24,32},{32,40},{40,48},{48,56},{56,6... | collective-permute-start | bytes 786440 | tf_op jit(solution)/shard_map/while/body/eval_jaxpr/ppermute | solution.py:38
  512.4 12.2 %collective-permute-start = (bf16[2,512,128]{2,1,0:T(8,128)(2,1)S(1)}, bf16[2,512,128]{2,1,0:T(8,128)(2,1)S(1)}, u32[]{:S(2)}, u32[]{:S(2)}) collective-permute-start(bf16[2,512,128]{2,1,0:T(8,128)(2,1)S(1)} %get-tuple-element.1172), channel_id=1, source_target_pairs={{248,0},{0,8},{8,16},{16,24},{24,32},{32,40},{40,48},{48,56},{56,6... | collective-permute-start | bytes 786440 | tf_op jit(solution)/shard_map/while/body/eval_jaxpr/ppermute | solution.py:38
  527.9 12.2 %collective-permute-start = (bf16[2,512,128]{2,1,0:T(8,128)(2,1)S(1)}, bf16[2,512,128]{2,1,0:T(8,128)(2,1)S(1)}, u32[]{:S(2)}, u32[]{:S(2)}) collective-permute-start(bf16[2,512,128]{2,1,0:T(8,128)(2,1)S(1)} %get-tuple-element.1172), channel_id=1, source_target_pairs={{248,0},{0,8},{8,16},{16,24},{24,32},{32,40},{40,48},{48,56},{56,6... | collective-permute-start | bytes 786440 | tf_op jit(solution)/shard_map/while/body/eval_jaxpr/ppermute | solution.py:38
  543.4 12.2 %collective-permute-start = (bf16[2,512,128]{2,1,0:T(8,128)(2,1)S(1)}, bf16[2,512,128]{2,1,0:T(8,128)(2,1)S(1)}, u32[]{:S(2)}, u32[]{:S(2)}) collective-permute-start(bf16[2,512,128]{2,1,0:T(8,128)(2,1)S(1)} %get-tuple-element.1172), channel_id=1, source_target_pairs={{248,0},{0,8},{8,16},{16,24},{24,32},{32,40},{40,48},{48,56},{56,6... | collective-permute-start | bytes 786440 | tf_op jit(solution)/shard_map/while/body/eval_jaxpr/ppermute | solution.py:38
  559.0 12.2 %collective-permute-start = (bf16[2,512,128]{2,1,0:T(8,128)(2,1)S(1)}, bf16[2,512,128]{2,1,0:T(8,128)(2,1)S(1)}, u32[]{:S(2)}, u32[]{:S(2)}) collective-permute-start(bf16[2,512,128]{2,1,0:T(8,128)(2,1)S(1)} %get-tuple-element.1172), channel_id=1, source_target_pairs={{248,0},{0,8},{8,16},{16,24},{24,32},{32,40},{40,48},{48,56},{56,6... | collective-permute-start | bytes 786440 | tf_op jit(solution)/shard_map/while/body/eval_jaxpr/ppermute | solution.py:38
  574.5 12.2 %collective-permute-start = (bf16[2,512,128]{2,1,0:T(8,128)(2,1)S(1)}, bf16[2,512,128]{2,1,0:T(8,128)(2,1)S(1)}, u32[]{:S(2)}, u32[]{:S(2)}) collective-permute-start(bf16[2,512,128]{2,1,0:T(8,128)(2,1)S(1)} %get-tuple-element.1172), channel_id=1, source_target_pairs={{248,0},{0,8},{8,16},{16,24},{24,32},{32,40},{40,48},{48,56},{56,6... | collective-permute-start | bytes 786440 | tf_op jit(solution)/shard_map/while/body/eval_jaxpr/ppermute | solution.py:38
  590.0 12.2 %collective-permute-start = (bf16[2,512,128]{2,1,0:T(8,128)(2,1)S(1)}, bf16[2,512,128]{2,1,0:T(8,128)(2,1)S(1)}, u32[]{:S(2)}, u32[]{:S(2)}) collective-permute-start(bf16[2,512,128]{2,1,0:T(8,128)(2,1)S(1)} %get-tuple-element.1172), channel_id=1, source_target_pairs={{248,0},{0,8},{8,16},{16,24},{24,32},{32,40},{40,48},{48,56},{56,6... | collective-permute-start | bytes 786440 | tf_op jit(solution)/shard_map/while/body/eval_jaxpr/ppermute | solution.py:38
  605.5 12.2 %collective-permute-start = (bf16[2,512,128]{2,1,0:T(8,128)(2,1)S(1)}, bf16[2,512,128]{2,1,0:T(8,128)(2,1)S(1)}, u32[]{:S(2)}, u32[]{:S(2)}) collective-permute-start(bf16[2,512,128]{2,1,0:T(8,128)(2,1)S(1)} %get-tuple-element.1172), channel_id=1, source_target_pairs={{248,0},{0,8},{8,16},{16,24},{24,32},{32,40},{40,48},{48,56},{56,6... | collective-permute-start | bytes 786440 | tf_op jit(solution)/shard_map/while/body/eval_jaxpr/ppermute | solution.py:38
  633.4 18.3 %collective-permute-start = (bf16[2,512,128]{2,1,0:T(8,128)(2,1)S(1)}, bf16[2,512,128]{2,1,0:T(8,128)(2,1)S(1)}, u32[]{:S(2)}, u32[]{:S(2)}) collective-permute-start(bf16[2,512,128]{2,1,0:T(8,128)(2,1)S(1)} %get-tuple-element.1172), channel_id=1, source_target_pairs={{248,0},{0,8},{8,16},{16,24},{24,32},{32,40},{40,48},{48,56},{56,6... | collective-permute-start | bytes 786440 | tf_op jit(solution)/shard_map/while/body/eval_jaxpr/ppermute | solution.py:38
  670.5 16.9 %collective-permute-start = (bf16[2,512,128]{2,1,0:T(8,128)(2,1)S(1)}, bf16[2,512,128]{2,1,0:T(8,128)(2,1)S(1)}, u32[]{:S(2)}, u32[]{:S(2)}) collective-permute-start(bf16[2,512,128]{2,1,0:T(8,128)(2,1)S(1)} %get-tuple-element.1172), channel_id=1, source_target_pairs={{248,0},{0,8},{8,16},{16,24},{24,32},{32,40},{40,48},{48,56},{56,6... | collective-permute-start | bytes 786440 | tf_op jit(solution)/shard_map/while/body/eval_jaxpr/ppermute | solution.py:38
  713.0 99.8 %reduce-scatter.5.cloned.1.call-start = ((), (), s32[]{:S(2)}) async-start(), calls=%async_computation.4 | async-start | bytes 1572864 | tf_op jit(solution)/shard_map/reduce_scatter | solution.py:46
  (8 other events, 440.9 us)
Sparse Core Ops, SparseCore 0:
  713.1 56.4 reduce-scatter.2
  772.1 40.6 reduce-scatter.4
